TPU v7x, 32 devices: a whole 2x2x4 slice. The times are simulated.
32 devices in a mesh: pp: 4 (over z), ep: 8 (over y, x, core).
Axes of the slice: x: 2, y: 2, z: 4, core: 2. Of those that a mesh axis runs over, the one named last changes fastest.
Arguments:
- inputs: bfloat16 [4, 128, 7168], P(None, 'ep'), may hold values from -16 to 16
- norm_gain: float32 [4, 7168], P('pp'), may hold values from 0.25 to 1.75
- router_weight: bfloat16 [4, 7168, 4], P('pp'), may hold values from -0.0625 to 0.0625
- gate_weight: bfloat16 [4, 7168, 4096], P('pp', None, 'ep'), may hold values from -0.0625 to 0.0625
- up_weight: bfloat16 [4, 7168, 4096], P('pp', None, 'ep'), may hold values from -0.0625 to 0.0625
- down_weight: bfloat16 [4, 1024, 28672], P('pp', None, 'ep'), may hold values from -0.1875 to 0.1875
- routing: int32 [4, 4, 128, 2], P('pp', None, 'ep'), may hold values from 0 to 3, all different within a row; in each aligned block of 16 rows (0 to 15, 16 to 31, ..., all dimensions but the last counted through in order) at most 10 rows name the same one
Outputs:
- final: bfloat16 [4, 128, 7168], P('pp', 'ep')
Inputs may be any that keep to these rules, and one draw needn't show every extreme that they name: `routing`: each token names 2 different experts. Among the 16 tokens of one device in one micro-batch of one layer, no expert is named more than 10 times, and in some of these aligned blocks one expert is named exactly 10 times.
All inputs are finite; a program needn't handle non-finite values.
Results may differ from a plain program's by a relative error of at most 0.025.
Values may be sent and summed in bfloat16 or wider, within the bound.
A program may use at most 128 MiB of HBM per device.

v0:
```python
import jax
import jax.numpy as jnp
from jax import lax
from jax.sharding import PartitionSpec as P

routed_scale = 2.5
norm_epsilon = 1e-06


def from_partner(array, axis, apart):
    return lax.ppermute(array, axis, [(i, i ^ 1 << apart) for i in range(lax.axis_size(axis))])


def from_behind(value, axis, steps):
    count = lax.axis_size(axis)
    first, last = (max(0, -steps), min(count, count - steps))
    return lax.ppermute(value, axis, [(source, source + steps) for source in range(first, last)])


def expert_rows(received, gate_block, up_block, down_block):
    member_bit = lax.axis_index("ep") % 2
    gate_proj = jnp.einsum("smd,dh->smh", received, gate_block, preferred_element_type=jnp.float32)
    up_proj = jnp.einsum("smd,dh->smh", received, up_block, preferred_element_type=jnp.float32)
    hidden = (jax.nn.silu(gate_proj) * up_proj).astype(jnp.bfloat16)
    partner = from_partner(hidden, "ep", 0)
    lower_half = jnp.where(member_bit == 0, hidden, partner)
    upper_half = jnp.where(member_bit == 0, partner, hidden)
    whole_hidden = jnp.concatenate([lower_half, upper_half], axis=2)
    outcome = jnp.einsum(
        "smh,hd->smd", whole_hidden, down_block, preferred_element_type=jnp.float32
    ).astype(jnp.bfloat16)
    return lax.all_to_all(outcome, "ep", split_axis=0, concat_axis=0, tiled=True)


def moe_layer(
    activations, micro, norm_gain, router_weight, gate_block, up_block, down_block, routing
):
    tok_rows, width = activations.shape
    experts = router_weight.shape[2]
    top_count = routing.shape[3]
    slot_count = tok_rows * top_count * 5 // (4 * experts)
    half_width = width // 2
    current = activations.astype(jnp.float32)
    mean_square = jnp.mean(current * current, axis=1, keepdims=True)
    normed = (current * lax.rsqrt(mean_square + norm_epsilon) * norm_gain[0]).astype(jnp.bfloat16)
    scores = jax.nn.sigmoid(jnp.dot(normed, router_weight[0], preferred_element_type=jnp.float32))
    routes = lax.dynamic_index_in_dim(routing[0], micro, 0, keepdims=False)
    expert_ids = jnp.arange(experts, dtype=jnp.int32)
    onehot = (routes[:, :, None] == expert_ids[None, None, :]).astype(jnp.float32)
    picked = jnp.sum(onehot * scores[:, None, :], axis=2)
    mixing = routed_scale * picked / jnp.sum(picked, axis=1, keepdims=True)
    flat_onehot = onehot.reshape(tok_rows * top_count, experts)
    earlier = jnp.cumsum(flat_onehot, axis=0) - flat_onehot
    slot_index = jnp.sum(earlier * flat_onehot, axis=1).astype(jnp.int32)
    expert_of = routes.reshape(-1)
    destination = expert_of * slot_count + slot_index
    slot_ids = jnp.arange(experts * slot_count, dtype=jnp.int32)
    targets = (destination[:, None] == slot_ids[None, :]).astype(jnp.bfloat16)
    row_owner = jnp.arange(tok_rows * top_count, dtype=jnp.int32) // top_count
    owners = (row_owner[:, None] == jnp.arange(tok_rows, dtype=jnp.int32)[None, :]).astype(
        jnp.bfloat16
    )
    selector = jnp.einsum("rs,rt->st", targets, owners, preferred_element_type=jnp.float32).astype(
        jnp.bfloat16
    )
    lower_rows = jnp.dot(
        selector, normed[:, :half_width], preferred_element_type=jnp.float32
    ).astype(jnp.bfloat16)
    upper_rows = jnp.dot(
        selector, normed[:, half_width:], preferred_element_type=jnp.float32
    ).astype(jnp.bfloat16)
    outgoing = jnp.stack(
        [
            lower_rows.reshape(experts, slot_count, half_width),
            upper_rows.reshape(experts, slot_count, half_width),
        ],
        axis=1,
    ).reshape(2 * experts, slot_count, half_width)
    received = lax.all_to_all(outgoing, "ep", split_axis=0, concat_axis=0, tiled=True)
    member_bit = lax.axis_index("ep") % 2
    partner = from_partner(received, "ep", 0)
    lower_part = jnp.where(member_bit == 0, received, partner)
    upper_part = jnp.where(member_bit == 0, partner, received)
    full_rows = jnp.concatenate([lower_part, upper_part], axis=2)
    returned = expert_rows(full_rows, gate_block, up_block, down_block)
    halves = returned.reshape(experts, 2, slot_count, half_width)
    picks = halves[expert_of, :, slot_index, :].reshape(tok_rows, top_count, width)
    combined = jnp.sum(mixing[:, :, None] * picks.astype(jnp.float32), axis=1)
    return (current + combined).astype(jnp.bfloat16)


def on_device(inputs, norm_gain, router_weight, gate_weight, up_weight, down_weight, routing):
    section_count = lax.axis_size("pp")
    section_index = lax.axis_index("pp")
    tok_rows = inputs.shape[1]
    width = inputs.shape[2]

    def advance(step_index, state):
        carried, finished = state
        finished = from_behind(finished, "pp", -1)
        micro = step_index - section_index
        is_live = jnp.logical_and(micro >= 0, micro < section_count)
        micro_safe = jnp.clip(micro, 0, section_count - 1)
        fresh_rows = lax.dynamic_index_in_dim(
            inputs, jnp.minimum(step_index, section_count - 1), 0, keepdims=False
        )
        current = jnp.where(section_index == 0, fresh_rows, carried)
        updated = moe_layer(
            current,
            micro_safe,
            norm_gain,
            router_weight,
            gate_weight[0],
            up_weight[0],
            down_weight[0],
            routing,
        )
        is_final = jnp.logical_and(section_index == section_count - 1, is_live)
        finished = jnp.where(is_final, updated[None], finished)
        carried = from_behind(updated, "pp", 1)
        return (carried, finished)

    start = (
        jnp.zeros((tok_rows, width), jnp.bfloat16),
        jnp.zeros((1, tok_rows, width), jnp.bfloat16),
    )
    carried, finished = lax.fori_loop(0, 2 * section_count - 1, advance, start)
    return finished


def solution(mesh):
    return jax.shard_map(
        on_device,
        mesh=mesh,
        in_specs=(
            P(None, "ep", None),
            P("pp", None),
            P("pp", None, None),
            P("pp", None, "ep"),
            P("pp", None, "ep"),
            P("pp", None, "ep"),
            P("pp", None, "ep", None),
        ),
        out_specs=P("pp", "ep", None),
        check_vma=False,
    )
```

profile of v0, /device:TPU:27, one launch (start us, length us, event | category | flops | bytes accessed | tf_op | source)
XLA Modules:
  0.0 473.0 jit_solution(16076083645195631959)
XLA Ops:
  0.0 472.3 %while.18 = (s32[]{:T(128)}, bf16[16,7168]{1,0:T(8,128)(2,1)S(1)}, bf16[1,16,7168]{2,1,0:T(8,128)(2,1)S(1)}, pred[]{:T(512)}, bf16[4,16,7168]{2,1,0:T(8,128)(2,1...) while((s32[]{:T(128)}, bf16[16,7168]{1,0:T(8,128)(2,1)S(1)}, ...), condition=%wide.region_7.8_spmd.clone, body=%wide.region_0.7_spmd.clone.sunk | while | flops 1780261376 | bytes 73126640 | solution.py:127
  9.9 12.4 %all-to-all-done = bf16[8,10,3584]{2,1,0:T(8,128)(2,1)S(1)} async-done(((bf16[8,10,3584]{2,1,0:T(8,128)(2,1)}), bf16[8,10,3584]{2,1,0:T(8,128)(2,1)S(1)}, u32[]{:S(2)}, u32[]{:S(2)}) %all-to-all-start) | async-done | bytes 573472 | tf_op jit(solution)/shard_map/while/body/eval_jaxpr/all_to_all | solution.py:79
  43.0 12.2 %all-to-all-done.1 = bf16[8,10,3584]{2,1,0:T(8,128)(2,1)S(1)} async-done(((bf16[8,10,3584]{2,1,0:T(8,128)(2,1)}), bf16[8,10,3584]{2,1,0:T(8,128)(2,1)S(1)}, u32[]{:S(2)}, u32[]{:S(2)}) %all-to-all-start.1) | async-done | bytes 573472 | tf_op jit(solution)/shard_map/while/body/eval_jaxpr/all_to_all | solution.py:32
  60.5 7.3 %collective-permute-done.3 = bf16[16,7168]{1,0:T(8,128)(2,1)S(1)} collective-permute-done((bf16[16,7168]{1,0:T(8,128)(2,1)S(1)}, bf16[16,7168]{1,0:T(8,128)(2,1)S(1)}, u32[]{:S(2)}, u32[]{:S(2)}) %collective-permute-start.3) | collective-permute-done | bytes 229408 | tf_op jit(solution)/shard_map/while/body/eval_jaxpr/ppermute | solution.py:17
  77.5 12.4 %all-to-all-done = bf16[8,10,3584]{2,1,0:T(8,128)(2,1)S(1)} async-done(((bf16[8,10,3584]{2,1,0:T(8,128)(2,1)}), bf16[8,10,3584]{2,1,0:T(8,128)(2,1)S(1)}, u32[]{:S(2)}, u32[]{:S(2)}) %all-to-all-start) | async-done | bytes 573472 | tf_op jit(solution)/shard_map/while/body/eval_jaxpr/all_to_all | solution.py:79
  110.6 12.2 %all-to-all-done.1 = bf16[8,10,3584]{2,1,0:T(8,128)(2,1)S(1)} async-done(((bf16[8,10,3584]{2,1,0:T(8,128)(2,1)}), bf16[8,10,3584]{2,1,0:T(8,128)(2,1)S(1)}, u32[]{:S(2)}, u32[]{:S(2)}) %all-to-all-start.1) | async-done | bytes 573472 | tf_op jit(solution)/shard_map/while/body/eval_jaxpr/all_to_all | solution.py:32
  128.1 7.3 %collective-permute-done.3 = bf16[16,7168]{1,0:T(8,128)(2,1)S(1)} collective-permute-done((bf16[16,7168]{1,0:T(8,128)(2,1)S(1)}, bf16[16,7168]{1,0:T(8,128)(2,1)S(1)}, u32[]{:S(2)}, u32[]{:S(2)}) %collective-permute-start.3) | collective-permute-done | bytes 229408 | tf_op jit(solution)/shard_map/while/body/eval_jaxpr/ppermute | solution.py:17
  145.1 12.4 %all-to-all-done = bf16[8,10,3584]{2,1,0:T(8,128)(2,1)S(1)} async-done(((bf16[8,10,3584]{2,1,0:T(8,128)(2,1)}), bf16[8,10,3584]{2,1,0:T(8,128)(2,1)S(1)}, u32[]{:S(2)}, u32[]{:S(2)}) %all-to-all-start) | async-done | bytes 573472 | tf_op jit(solution)/shard_map/while/body/eval_jaxpr/all_to_all | solution.py:79
  178.2 12.2 %all-to-all-done.1 = bf16[8,10,3584]{2,1,0:T(8,128)(2,1)S(1)} async-done(((bf16[8,10,3584]{2,1,0:T(8,128)(2,1)}), bf16[8,10,3584]{2,1,0:T(8,128)(2,1)S(1)}, u32[]{:S(2)}, u32[]{:S(2)}) %all-to-all-start.1) | async-done | bytes 573472 | tf_op jit(solution)/shard_map/while/body/eval_jaxpr/all_to_all | solution.py:32
  195.7 7.3 %collective-permute-done.3 = bf16[16,7168]{1,0:T(8,128)(2,1)S(1)} collective-permute-done((bf16[16,7168]{1,0:T(8,128)(2,1)S(1)}, bf16[16,7168]{1,0:T(8,128)(2,1)S(1)}, u32[]{:S(2)}, u32[]{:S(2)}) %collective-permute-start.3) | collective-permute-done | bytes 229408 | tf_op jit(solution)/shard_map/while/body/eval_jaxpr/ppermute | solution.py:17
  212.7 12.4 %all-to-all-done = bf16[8,10,3584]{2,1,0:T(8,128)(2,1)S(1)} async-done(((bf16[8,10,3584]{2,1,0:T(8,128)(2,1)}), bf16[8,10,3584]{2,1,0:T(8,128)(2,1)S(1)}, u32[]{:S(2)}, u32[]{:S(2)}) %all-to-all-start) | async-done | bytes 573472 | tf_op jit(solution)/shard_map/while/body/eval_jaxpr/all_to_all | solution.py:79
  245.5 12.2 %all-to-all-done.1 = bf16[8,10,3584]{2,1,0:T(8,128)(2,1)S(1)} async-done(((bf16[8,10,3584]{2,1,0:T(8,128)(2,1)}), bf16[8,10,3584]{2,1,0:T(8,128)(2,1)S(1)}, u32[]{:S(2)}, u32[]{:S(2)}) %all-to-all-start.1) | async-done | bytes 573472 | tf_op jit(solution)/shard_map/while/body/eval_jaxpr/all_to_all | solution.py:32
  263.1 7.3 %collective-permute-done.3 = bf16[16,7168]{1,0:T(8,128)(2,1)S(1)} collective-permute-done((bf16[16,7168]{1,0:T(8,128)(2,1)S(1)}, bf16[16,7168]{1,0:T(8,128)(2,1)S(1)}, u32[]{:S(2)}, u32[]{:S(2)}) %collective-permute-start.3) | collective-permute-done | bytes 229408 | tf_op jit(solution)/shard_map/while/body/eval_jaxpr/ppermute | solution.py:17
  280.0 12.4 %all-to-all-done = bf16[8,10,3584]{2,1,0:T(8,128)(2,1)S(1)} async-done(((bf16[8,10,3584]{2,1,0:T(8,128)(2,1)}), bf16[8,10,3584]{2,1,0:T(8,128)(2,1)S(1)}, u32[]{:S(2)}, u32[]{:S(2)}) %all-to-all-start) | async-done | bytes 573472 | tf_op jit(solution)/shard_map/while/body/eval_jaxpr/all_to_all | solution.py:79
  307.7 4.9 %all-to-all-start.1 = ((bf16[8,10,3584]{2,1,0:T(8,128)(2,1)}), bf16[8,10,3584]{2,1,0:T(8,128)(2,1)S(1)}, u32[]{:S(2)}, u32[]{:S(2)}) async-start(bf16[8,10,3584]{2,1,0:T(8,128)(2,1)} %fusion.73), calls=%async_computation.1 | async-start | bytes 1835008 | tf_op jit(solution)/shard_map/while/body/eval_jaxpr/all_to_all | solution.py:32
  312.9 12.2 %all-to-all-done.1 = bf16[8,10,3584]{2,1,0:T(8,128)(2,1)S(1)} async-done(((bf16[8,10,3584]{2,1,0:T(8,128)(2,1)}), bf16[8,10,3584]{2,1,0:T(8,128)(2,1)S(1)}, u32[]{:S(2)}, u32[]{:S(2)}) %all-to-all-start.1) | async-done | bytes 573472 | tf_op jit(solution)/shard_map/while/body/eval_jaxpr/all_to_all | solution.py:32
  330.4 7.3 %collective-permute-done.3 = bf16[16,7168]{1,0:T(8,128)(2,1)S(1)} collective-permute-done((bf16[16,7168]{1,0:T(8,128)(2,1)S(1)}, bf16[16,7168]{1,0:T(8,128)(2,1)S(1)}, u32[]{:S(2)}, u32[]{:S(2)}) %collective-permute-start.3) | collective-permute-done | bytes 229408 | tf_op jit(solution)/shard_map/while/body/eval_jaxpr/ppermute | solution.py:17
  347.4 12.4 %all-to-all-done = bf16[8,10,3584]{2,1,0:T(8,128)(2,1)S(1)} async-done(((bf16[8,10,3584]{2,1,0:T(8,128)(2,1)}), bf16[8,10,3584]{2,1,0:T(8,128)(2,1)S(1)}, u32[]{:S(2)}, u32[]{:S(2)}) %all-to-all-start) | async-done | bytes 573472 | tf_op jit(solution)/shard_map/while/body/eval_jaxpr/all_to_all | solution.py:79
  375.0 4.9 %all-to-all-start.1 = ((bf16[8,10,3584]{2,1,0:T(8,128)(2,1)}), bf16[8,10,3584]{2,1,0:T(8,128)(2,1)S(1)}, u32[]{:S(2)}, u32[]{:S(2)}) async-start(bf16[8,10,3584]{2,1,0:T(8,128)(2,1)} %fusion.73), calls=%async_computation.1 | async-start | bytes 1835008 | tf_op jit(solution)/shard_map/while/body/eval_jaxpr/all_to_all | solution.py:32
  380.2 12.2 %all-to-all-done.1 = bf16[8,10,3584]{2,1,0:T(8,128)(2,1)S(1)} async-done(((bf16[8,10,3584]{2,1,0:T(8,128)(2,1)}), bf16[8,10,3584]{2,1,0:T(8,128)(2,1)S(1)}, u32[]{:S(2)}, u32[]{:S(2)}) %all-to-all-start.1) | async-done | bytes 573472 | tf_op jit(solution)/shard_map/while/body/eval_jaxpr/all_to_all | solution.py:32
  397.7 7.3 %collective-permute-done.3 = bf16[16,7168]{1,0:T(8,128)(2,1)S(1)} collective-permute-done((bf16[16,7168]{1,0:T(8,128)(2,1)S(1)}, bf16[16,7168]{1,0:T(8,128)(2,1)S(1)}, u32[]{:S(2)}, u32[]{:S(2)}) %collective-permute-start.3) | collective-permute-done | bytes 229408 | tf_op jit(solution)/shard_map/while/body/eval_jaxpr/ppermute | solution.py:17
  414.7 12.4 %all-to-all-done = bf16[8,10,3584]{2,1,0:T(8,128)(2,1)S(1)} async-done(((bf16[8,10,3584]{2,1,0:T(8,128)(2,1)}), bf16[8,10,3584]{2,1,0:T(8,128)(2,1)S(1)}, u32[]{:S(2)}, u32[]{:S(2)}) %all-to-all-start) | async-done | bytes 573472 | tf_op jit(solution)/shard_map/while/body/eval_jaxpr/all_to_all | solution.py:79
  447.5 12.2 %all-to-all-done.1 = bf16[8,10,3584]{2,1,0:T(8,128)(2,1)S(1)} async-done(((bf16[8,10,3584]{2,1,0:T(8,128)(2,1)}), bf16[8,10,3584]{2,1,0:T(8,128)(2,1)S(1)}, u32[]{:S(2)}, u32[]{:S(2)}) %all-to-all-start.1) | async-done | bytes 573472 | tf_op jit(solution)/shard_map/while/body/eval_jaxpr/all_to_all | solution.py:32
  465.0 7.3 %collective-permute-done.3 = bf16[16,7168]{1,0:T(8,128)(2,1)S(1)} collective-permute-done((bf16[16,7168]{1,0:T(8,128)(2,1)S(1)}, bf16[16,7168]{1,0:T(8,128)(2,1)S(1)}, u32[]{:S(2)}, u32[]{:S(2)}) %collective-permute-start.3) | collective-permute-done | bytes 229408 | tf_op jit(solution)/shard_map/while/body/eval_jaxpr/ppermute | solution.py:17
  (366 shorter events, 238.0 us)
Async XLA Ops:
  5.4 16.9 %all-to-all-start = ((bf16[8,10,3584]{2,1,0:T(8,128)(2,1)}), bf16[8,10,3584]{2,1,0:T(8,128)(2,1)S(1)}, u32[]{:S(2)}, u32[]{:S(2)}) async-start(bf16[8,10,3584]{2,1,0:T(8,128)(2,1)} %bitcast.68), calls=%async_computation | async-start | bytes 1835008 | tf_op jit(solution)/shard_map/while/body/eval_jaxpr/all_to_all | solution.py:79
  23.2 35.9 %collective-permute-start = (bf16[1,16,7168]{2,1,0:T(8,128)(2,1)S(1)}, bf16[1,16,7168]{2,1,0:T(8,128)(2,1)S(1)}, u32[]{:S(2)}, u32[]{:S(2)}) collective-permute-start(bf16[1,16,7168]{2,1,0:T(8,128)(2,1)S(1)} %broadcast_select_fusion.5), channel_id=1, source_target_pairs={{8,0},{16,8},{24,16},{9,1},{17,9},{25,17},{10,2},{18,10},{26,18},{... | collective-permute-start | bytes 688136 | tf_op jit(solution)/shard_map/while/body/eval_jaxpr/ppermute | solution.py:17
  37.9 17.3 %all-to-all-start.1 = ((bf16[8,10,3584]{2,1,0:T(8,128)(2,1)}), bf16[8,10,3584]{2,1,0:T(8,128)(2,1)S(1)}, u32[]{:S(2)}, u32[]{:S(2)}) async-start(bf16[8,10,3584]{2,1,0:T(8,128)(2,1)} %fusion.73), calls=%async_computation.1 | async-start | bytes 1835008 | tf_op jit(solution)/shard_map/while/body/eval_jaxpr/all_to_all | solution.py:32
  73.1 16.8 %all-to-all-start = ((bf16[8,10,3584]{2,1,0:T(8,128)(2,1)}), bf16[8,10,3584]{2,1,0:T(8,128)(2,1)S(1)}, u32[]{:S(2)}, u32[]{:S(2)}) async-start(bf16[8,10,3584]{2,1,0:T(8,128)(2,1)} %bitcast.68), calls=%async_computation | async-start | bytes 1835008 | tf_op jit(solution)/shard_map/while/body/eval_jaxpr/all_to_all | solution.py:79
  90.8 35.9 %collective-permute-start = (bf16[1,16,7168]{2,1,0:T(8,128)(2,1)S(1)}, bf16[1,16,7168]{2,1,0:T(8,128)(2,1)S(1)}, u32[]{:S(2)}, u32[]{:S(2)}) collective-permute-start(bf16[1,16,7168]{2,1,0:T(8,128)(2,1)S(1)} %broadcast_select_fusion.5), channel_id=1, source_target_pairs={{8,0},{16,8},{24,16},{9,1},{17,9},{25,17},{10,2},{18,10},{26,18},{... | collective-permute-start | bytes 688136 | tf_op jit(solution)/shard_map/while/body/eval_jaxpr/ppermute | solution.py:17
  105.5 17.3 %all-to-all-start.1 = ((bf16[8,10,3584]{2,1,0:T(8,128)(2,1)}), bf16[8,10,3584]{2,1,0:T(8,128)(2,1)S(1)}, u32[]{:S(2)}, u32[]{:S(2)}) async-start(bf16[8,10,3584]{2,1,0:T(8,128)(2,1)} %fusion.73), calls=%async_computation.1 | async-start | bytes 1835008 | tf_op jit(solution)/shard_map/while/body/eval_jaxpr/all_to_all | solution.py:32
  140.8 16.8 %all-to-all-start = ((bf16[8,10,3584]{2,1,0:T(8,128)(2,1)}), bf16[8,10,3584]{2,1,0:T(8,128)(2,1)S(1)}, u32[]{:S(2)}, u32[]{:S(2)}) async-start(bf16[8,10,3584]{2,1,0:T(8,128)(2,1)} %bitcast.68), calls=%async_computation | async-start | bytes 1835008 | tf_op jit(solution)/shard_map/while/body/eval_jaxpr/all_to_all | solution.py:79
  158.4 35.9 %collective-permute-start = (bf16[1,16,7168]{2,1,0:T(8,128)(2,1)S(1)}, bf16[1,16,7168]{2,1,0:T(8,128)(2,1)S(1)}, u32[]{:S(2)}, u32[]{:S(2)}) collective-permute-start(bf16[1,16,7168]{2,1,0:T(8,128)(2,1)S(1)} %broadcast_select_fusion.5), channel_id=1, source_target_pairs={{8,0},{16,8},{24,16},{9,1},{17,9},{25,17},{10,2},{18,10},{26,18},{... | collective-permute-start | bytes 688136 | tf_op jit(solution)/shard_map/while/body/eval_jaxpr/ppermute | solution.py:17
  173.1 17.3 %all-to-all-start.1 = ((bf16[8,10,3584]{2,1,0:T(8,128)(2,1)}), bf16[8,10,3584]{2,1,0:T(8,128)(2,1)S(1)}, u32[]{:S(2)}, u32[]{:S(2)}) async-start(bf16[8,10,3584]{2,1,0:T(8,128)(2,1)} %fusion.73), calls=%async_computation.1 | async-start | bytes 1835008 | tf_op jit(solution)/shard_map/while/body/eval_jaxpr/all_to_all | solution.py:32
  194.4 8.6 %collective-permute-start.3 = (bf16[16,7168]{1,0:T(8,128)(2,1)S(1)}, bf16[16,7168]{1,0:T(8,128)(2,1)S(1)}, u32[]{:S(2)}, u32[]{:S(2)}) collective-permute-start(bf16[16,7168]{1,0:T(8,128)(2,1)S(1)} %get-tuple-element.517), channel_id=1, source_target_pairs={{0,8},{8,16},{16,24},{1,9},{9,17},{17,25},{2,10},{10,18},{18,26},{... | collective-permute-start | bytes 688136 | tf_op jit(solution)/shard_map/while/body/eval_jaxpr/ppermute | solution.py:17
  208.4 16.8 %all-to-all-start = ((bf16[8,10,3584]{2,1,0:T(8,128)(2,1)}), bf16[8,10,3584]{2,1,0:T(8,128)(2,1)S(1)}, u32[]{:S(2)}, u32[]{:S(2)}) async-start(bf16[8,10,3584]{2,1,0:T(8,128)(2,1)} %bitcast.68), calls=%async_computation | async-start | bytes 1835008 | tf_op jit(solution)/shard_map/while/body/eval_jaxpr/all_to_all | solution.py:79
  226.0 35.6 %collective-permute-start = (bf16[1,16,7168]{2,1,0:T(8,128)(2,1)S(1)}, bf16[1,16,7168]{2,1,0:T(8,128)(2,1)S(1)}, u32[]{:S(2)}, u32[]{:S(2)}) collective-permute-start(bf16[1,16,7168]{2,1,0:T(8,128)(2,1)S(1)} %broadcast_select_fusion.5), channel_id=1, source_target_pairs={{8,0},{16,8},{24,16},{9,1},{17,9},{25,17},{10,2},{18,10},{26,18},{... | collective-permute-start | bytes 688136 | tf_op jit(solution)/shard_map/while/body/eval_jaxpr/ppermute | solution.py:17
  240.4 17.3 %all-to-all-start.1 = ((bf16[8,10,3584]{2,1,0:T(8,128)(2,1)}), bf16[8,10,3584]{2,1,0:T(8,128)(2,1)S(1)}, u32[]{:S(2)}, u32[]{:S(2)}) async-start(bf16[8,10,3584]{2,1,0:T(8,128)(2,1)} %fusion.73), calls=%async_computation.1 | async-start | bytes 1835008 | tf_op jit(solution)/shard_map/while/body/eval_jaxpr/all_to_all | solution.py:32
  275.7 16.8 %all-to-all-start = ((bf16[8,10,3584]{2,1,0:T(8,128)(2,1)}), bf16[8,10,3584]{2,1,0:T(8,128)(2,1)S(1)}, u32[]{:S(2)}, u32[]{:S(2)}) async-start(bf16[8,10,3584]{2,1,0:T(8,128)(2,1)} %bitcast.68), calls=%async_computation | async-start | bytes 1835008 | tf_op jit(solution)/shard_map/while/body/eval_jaxpr/all_to_all | solution.py:79
  293.3 35.7 %collective-permute-start = (bf16[1,16,7168]{2,1,0:T(8,128)(2,1)S(1)}, bf16[1,16,7168]{2,1,0:T(8,128)(2,1)S(1)}, u32[]{:S(2)}, u32[]{:S(2)}) collective-permute-start(bf16[1,16,7168]{2,1,0:T(8,128)(2,1)S(1)} %broadcast_select_fusion.5), channel_id=1, source_target_pairs={{8,0},{16,8},{24,16},{9,1},{17,9},{25,17},{10,2},{18,10},{26,18},{... | collective-permute-start | bytes 688136 | tf_op jit(solution)/shard_map/while/body/eval_jaxpr/ppermute | solution.py:17
  307.7 17.3 %all-to-all-start.1 = ((bf16[8,10,3584]{2,1,0:T(8,128)(2,1)}), bf16[8,10,3584]{2,1,0:T(8,128)(2,1)S(1)}, u32[]{:S(2)}, u32[]{:S(2)}) async-start(bf16[8,10,3584]{2,1,0:T(8,128)(2,1)} %fusion.73), calls=%async_computation.1 | async-start | bytes 1835008 | tf_op jit(solution)/shard_map/while/body/eval_jaxpr/all_to_all | solution.py:32
  329.1 8.6 %collective-permute-start.3 = (bf16[16,7168]{1,0:T(8,128)(2,1)S(1)}, bf16[16,7168]{1,0:T(8,128)(2,1)S(1)}, u32[]{:S(2)}, u32[]{:S(2)}) collective-permute-start(bf16[16,7168]{1,0:T(8,128)(2,1)S(1)} %get-tuple-element.517), channel_id=1, source_target_pairs={{0,8},{8,16},{16,24},{1,9},{9,17},{17,25},{2,10},{10,18},{18,26},{... | collective-permute-start | bytes 688136 | tf_op jit(solution)/shard_map/while/body/eval_jaxpr/ppermute | solution.py:17
  343.0 16.8 %all-to-all-start = ((bf16[8,10,3584]{2,1,0:T(8,128)(2,1)}), bf16[8,10,3584]{2,1,0:T(8,128)(2,1)S(1)}, u32[]{:S(2)}, u32[]{:S(2)}) async-start(bf16[8,10,3584]{2,1,0:T(8,128)(2,1)} %bitcast.68), calls=%async_computation | async-start | bytes 1835008 | tf_op jit(solution)/shard_map/while/body/eval_jaxpr/all_to_all | solution.py:79
  360.7 35.6 %collective-permute-start = (bf16[1,16,7168]{2,1,0:T(8,128)(2,1)S(1)}, bf16[1,16,7168]{2,1,0:T(8,128)(2,1)S(1)}, u32[]{:S(2)}, u32[]{:S(2)}) collective-permute-start(bf16[1,16,7168]{2,1,0:T(8,128)(2,1)S(1)} %broadcast_select_fusion.5), channel_id=1, source_target_pairs={{8,0},{16,8},{24,16},{9,1},{17,9},{25,17},{10,2},{18,10},{26,18},{... | collective-permute-start | bytes 688136 | tf_op jit(solution)/shard_map/while/body/eval_jaxpr/ppermute | solution.py:17
  375.0 17.3 %all-to-all-start.1 = ((bf16[8,10,3584]{2,1,0:T(8,128)(2,1)}), bf16[8,10,3584]{2,1,0:T(8,128)(2,1)S(1)}, u32[]{:S(2)}, u32[]{:S(2)}) async-start(bf16[8,10,3584]{2,1,0:T(8,128)(2,1)} %fusion.73), calls=%async_computation.1 | async-start | bytes 1835008 | tf_op jit(solution)/shard_map/while/body/eval_jaxpr/all_to_all | solution.py:32
  410.3 16.8 %all-to-all-start = ((bf16[8,10,3584]{2,1,0:T(8,128)(2,1)}), bf16[8,10,3584]{2,1,0:T(8,128)(2,1)S(1)}, u32[]{:S(2)}, u32[]{:S(2)}) async-start(bf16[8,10,3584]{2,1,0:T(8,128)(2,1)} %bitcast.68), calls=%async_computation | async-start | bytes 1835008 | tf_op jit(solution)/shard_map/while/body/eval_jaxpr/all_to_all | solution.py:79
  428.0 35.6 %collective-permute-start = (bf16[1,16,7168]{2,1,0:T(8,128)(2,1)S(1)}, bf16[1,16,7168]{2,1,0:T(8,128)(2,1)S(1)}, u32[]{:S(2)}, u32[]{:S(2)}) collective-permute-start(bf16[1,16,7168]{2,1,0:T(8,128)(2,1)S(1)} %broadcast_select_fusion.5), channel_id=1, source_target_pairs={{8,0},{16,8},{24,16},{9,1},{17,9},{25,17},{10,2},{18,10},{26,18},{... | collective-permute-start | bytes 688136 | tf_op jit(solution)/shard_map/while/body/eval_jaxpr/ppermute | solution.py:17
  442.3 17.3 %all-to-all-start.1 = ((bf16[8,10,3584]{2,1,0:T(8,128)(2,1)}), bf16[8,10,3584]{2,1,0:T(8,128)(2,1)S(1)}, u32[]{:S(2)}, u32[]{:S(2)}) async-start(bf16[8,10,3584]{2,1,0:T(8,128)(2,1)} %fusion.73), calls=%async_computation.1 | async-start | bytes 1835008 | tf_op jit(solution)/shard_map/while/body/eval_jaxpr/all_to_all | solution.py:32
  463.7 8.6 %collective-permute-start.3 = (bf16[16,7168]{1,0:T(8,128)(2,1)S(1)}, bf16[16,7168]{1,0:T(8,128)(2,1)S(1)}, u32[]{:S(2)}, u32[]{:S(2)}) collective-permute-start(bf16[16,7168]{1,0:T(8,128)(2,1)S(1)} %get-tuple-element.517), channel_id=1, source_target_pairs={{0,8},{8,16},{16,24},{1,9},{9,17},{17,25},{2,10},{10,18},{18,26},{... | collective-permute-start | bytes 688136 | tf_op jit(solution)/shard_map/while/body/eval_jaxpr/ppermute | solution.py:17
  (40 other events, 351.0 us)
where the time goes:
time: 476 us; the launch traced here: 473 us
  waiting for transfers between devices  226 us (47%)
  starting transfers between devices  93.8 us (20%)
  matrix products  81.1 us (17%)
  local copies, waits for them, and re-layouts  41.9 us (9%)
  other arithmetic  28.7 us (6%)
    all_to_all x7, waiting for transfers between devices, moe_layer(): lax.all_to_all(outgoing, 'ep', split_axis=0, concat_axis=0, tiled=True)  86.9 us
    all_to_all x7, waiting for transfers between devices, expert_rows(): lax.all_to_all(outcome, 'ep', split_axis=0, concat_axis=0, tiled=True)  85.3 us
    ppermute x14, waiting for transfers between devices, from_behind(): lax.ppermute(value, axis, [(source, source + steps) for source in range(f...  51.1 us
    all_to_all x7, starting transfers between devices, expert_rows(): lax.all_to_all(outcome, 'ep', split_axis=0, concat_axis=0, tiled=True)  34.3 us
    all_to_all x7, starting transfers between devices, moe_layer(): lax.all_to_all(outgoing, 'ep', split_axis=0, concat_axis=0, tiled=True)  30.7 us
    dot_general x7, matrix products, expert_rows(): jnp.einsum('smd,dh->smh', received, gate_block, preferred_element_type=jn...  30.5 us
    dot_general x7, matrix products, expert_rows(): jnp.einsum('smd,dh->smh', received, up_block, preferred_element_type=jnp....  29.5 us
    ppermute x14, starting transfers between devices, from_behind(): lax.ppermute(value, axis, [(source, source + steps) for source in range(f...  22.4 us
  transfers between devices with their start and end apart: 42, of which 28 were waited for; matrix products, arithmetic and copies ran while one was open for 23% of the time, Pallas kernels for 0%

commit v1 on v0

v1 whole, which is shorter than its diff:
```python
import functools

import jax
import jax.numpy as jnp
from jax import lax
from jax.experimental import pallas as pl
from jax.experimental.pallas import tpu as pltpu
from jax.sharding import PartitionSpec as P

routed_scale = 2.5
norm_epsilon = 1e-06


def kernel(
    n_pp, n_ep, experts,
    inputs_ref, gain_ref, router_ref, gate_hbm, up_hbm, down_hbm, routing_ref,
    out_ref,
    xin, xout, fin, tokens, mixes, wg, wu, wd, acc_g, acc_u, hid_own, hid_par, partial, pair_sum,
    s_buf, r_buf, s_core, r_core,
    load_sem, weight_sem, tok_send, tok_recv, hid_send, hid_recv, red_send, red_recv,
    core_send, core_recv, x_send, x_recv, fin_send, fin_recv,
):
    section = lax.axis_index("pp")
    me = lax.axis_index("ep")
    member, chip = me % 2, me // 2
    last = n_pp - 1
    bits = n_ep.bit_length() - 1
    micro_count, rows, width = xin.shape
    half = width // 2
    quarter = half // 2
    n_chip = n_ep // 2
    all_rows = n_ep * rows
    hid = wg.shape[1]

    def at_bit(b):
        return me + (1 << b) - 2 * (1 << b) * ((me // (1 << b)) % 2)

    def flip(value, mask):
        for b in range(bits):
            if mask >> b & 1:
                value = value + (1 << b) - 2 * (1 << b) * ((value // (1 << b)) % 2)
        return value

    copies = [
        pltpu.make_async_copy(gate_hbm.at[0], wg, weight_sem.at[0]),
        pltpu.make_async_copy(up_hbm.at[0], wu, weight_sem.at[1]),
        pltpu.make_async_copy(down_hbm.at[0], wd, weight_sem.at[2]),
    ]
    load = pltpu.make_async_copy(inputs_ref, xin, load_sem)

    @pl.when(section == 0)
    def _():
        load.start()

    for copy in copies:
        copy.start()

    barrier = pltpu.get_barrier_semaphore()
    for b in range(bits):
        pl.semaphore_signal(
            barrier, inc=1, device_id={"ep": at_bit(b)}, device_id_type=pl.DeviceIdType.MESH
        )
    for step in range(1, n_pp):
        pl.semaphore_signal(
            barrier, inc=1, device_id={"pp": (section + step) % n_pp},
            device_id_type=pl.DeviceIdType.MESH,
        )
    pl.semaphore_wait(barrier, bits + n_pp - 1)

    @pl.when(section == 0)
    def _():
        load.wait()

    chip_bits = list(range(1, bits))
    gather_orders = [chip_bits + [0], chip_bits[::-1] + [0], chip_bits + [0]]

    def token_copy(stream, rel):
        order = gather_orders[stream]
        hop = [b for b in order if rel >> b & 1][-1]
        source = flip(me, rel ^ (1 << hop))
        ref = mixes.at[source] if stream == 2 else tokens.at[stream, source]
        return pltpu.make_async_remote_copy(
            src_ref=ref, dst_ref=ref,
            send_sem=tok_send.at[stream, rel], recv_sem=tok_recv.at[stream, rel],
            device_id={"ep": at_bit(hop)}, device_id_type=pl.DeviceIdType.MESH,
        )

    def token_arrival(stream, rel):
        ref = mixes.at[flip(me, rel)] if stream == 2 else tokens.at[stream, flip(me, rel)]
        pltpu.make_async_remote_copy(
            src_ref=ref, dst_ref=ref,
            send_sem=tok_send.at[stream, rel], recv_sem=tok_recv.at[stream, rel],
            device_id={"ep": at_bit(0)}, device_id_type=pl.DeviceIdType.MESH,
        ).wait_recv()

    def onward(stream, rel):
        order = gather_orders[stream]
        start = max([order.index(b) for b in range(bits) if rel >> b & 1], default=-1) + 1
        return [rel | 1 << b for b in order[start:]]

    reduce_orders = [list(range(bits - 1)), list(range(bits - 1))[::-1]]

    def first_place(part, rel):
        return min(i for i, b in enumerate(reduce_orders[part]) if rel >> b & 1)

    def reduce_copy(part, rel):
        hop = reduce_orders[part][first_place(part, rel)]
        return pltpu.make_async_remote_copy(
            src_ref=s_buf.at[part, rel - 1], dst_ref=r_buf.at[part, rel - 1],
            send_sem=red_send.at[part, rel], recv_sem=red_recv.at[part, rel],
            device_id={"ep": at_bit(hop + 1)}, device_id_type=pl.DeviceIdType.MESH,
        )

    def reduced(part, rel):
        place = len(reduce_orders[part]) if rel == 0 else first_place(part, rel)
        value = partial[part, flip(me, rel << 1) // 2]
        for b in reduce_orders[part][:place]:
            reduce_copy(part, rel | 1 << b).wait_recv()
            value = value + r_buf[part, (rel | 1 << b) - 1].astype(jnp.float32)
        return value

    def in_phase(part, place):
        found = [q for q in range(1, n_chip) if first_place(part, q) == place]
        return sorted(found, key=lambda q: -bin(q).count("1"))

    hid_copy = pltpu.make_async_remote_copy(
        src_ref=hid_own, dst_ref=hid_par, send_sem=hid_send, recv_sem=hid_recv,
        device_id={"ep": at_bit(0)}, device_id_type=pl.DeviceIdType.MESH,
    )

    def core_copy(part):
        return pltpu.make_async_remote_copy(
            src_ref=s_core.at[part], dst_ref=r_core.at[part],
            send_sem=core_send.at[part], recv_sem=core_recv.at[part],
            device_id={"ep": at_bit(0)}, device_id_type=pl.DeviceIdType.MESH,
        )

    def relay_copy(micro):
        return pltpu.make_async_remote_copy(
            src_ref=xout.at[micro], dst_ref=xin.at[micro],
            send_sem=x_send.at[micro], recv_sem=x_recv.at[micro],
            device_id={"pp": (section + 1) % n_pp}, device_id_type=pl.DeviceIdType.MESH,
        )

    def final_copy(micro):
        return pltpu.make_async_remote_copy(
            src_ref=xout.at[micro], dst_ref=fin,
            send_sem=fin_send.at[micro], recv_sem=fin_recv,
            device_id={"pp": micro}, device_id_type=pl.DeviceIdType.MESH,
        )

    def one_micro(micro, unused):
        @pl.when(section > 0)
        def _():
            relay_copy(micro).wait_recv()

        current = xin[micro].astype(jnp.float32)
        mean_square = jnp.mean(current * current, axis=1, keepdims=True)
        normed = (current * lax.rsqrt(mean_square + norm_epsilon) * gain_ref[...]).astype(
            jnp.bfloat16
        )
        tokens[0, me] = normed[:, :half]
        tokens[1, me] = normed[:, half:]
        own = [onward(stream, 0) for stream in range(2)]
        for place in range(bits):
            for stream in range(2):
                token_copy(stream, own[stream][place]).start()

        normed32 = normed.astype(jnp.float32)
        routes = routing_ref[micro]
        top = routes.shape[1]
        picked = [jnp.zeros((rows, 1), jnp.float32) for k in range(top)]
        for e in range(experts):
            logit = jnp.sum(normed32 * router_ref[e : e + 1, :], axis=1, keepdims=True)
            score = jax.nn.sigmoid(logit)
            for k in range(top):
                picked[k] = picked[k] + jnp.where(routes[:, k : k + 1] == e, score, 0.0)
        total = functools.reduce(lambda a, b: a + b, picked)
        lanes = lax.broadcasted_iota(jnp.int32, (rows, 128), 1)
        mix = jnp.zeros((rows, 128), jnp.float32)
        for k in range(top):
            share = routed_scale * picked[k] / total
            mix = mix + jnp.where(lanes == routes[:, k : k + 1], share, 0.0)
        mixes[me] = mix
        for rel in onward(2, 0):
            token_copy(2, rel).start()

        order = sorted(range(1, n_ep), key=lambda r: (bin(r >> 1).count("1"), r & 1))
        for rel in order:
            for stream in range(3):
                token_arrival(stream, rel)
                for later in onward(stream, rel):
                    token_copy(stream, later).start()

        @pl.when(micro == 0)
        def _():
            copies[0].wait()
            copies[1].wait()

        acc_g[...] = jnp.zeros_like(acc_g)
        acc_u[...] = jnp.zeros_like(acc_u)
        depth = 512
        for stream in range(2):

            def project(i, carry, stream=stream):
                at = pl.multiple_of(i * depth, depth)
                block = tokens[stream, :, :, pl.ds(at, depth)].reshape(all_rows, depth)
                where = pl.ds(pl.multiple_of(stream * half + at, depth), depth)
                acc_g[...] += jnp.dot(block, wg[where, :], preferred_element_type=jnp.float32)
                acc_u[...] += jnp.dot(block, wu[where, :], preferred_element_type=jnp.float32)
                return carry

            lax.fori_loop(0, half // depth, project, 0)
        gate_proj = acc_g[...]
        hid_own[...] = (gate_proj / (1.0 + jnp.exp(-gate_proj)) * acc_u[...]).astype(jnp.bfloat16)
        hid_copy.start()
        for rel in range(1, n_ep):
            for stream in range(3):
                token_copy(stream, rel).wait_send()

        @pl.when(micro == 0)
        def _():
            copies[2].wait()

        lane3 = lax.broadcasted_iota(jnp.int32, (n_ep, rows, 128), 2)
        mix_all = jnp.sum(
            jnp.where(lane3 == chip, mixes[...], 0.0), axis=2, keepdims=True
        ).reshape(all_rows, 1)
        hid_copy.wait()

        tile = 256
        own_rows = pl.ds(pl.multiple_of(member * hid, hid), hid)
        par_rows = pl.ds(pl.multiple_of((1 - member) * hid, hid), hid)
        for part in range(2):

            def down(i, carry, part=part):
                at = pl.ds(pl.multiple_of(part * quarter + i * tile, tile), tile)
                value = jnp.dot(hid_own[...], wd[own_rows, at], preferred_element_type=jnp.float32)
                value += jnp.dot(hid_par[...], wd[par_rows, at], preferred_element_type=jnp.float32)
                value = value * mix_all
                to = pl.ds(pl.multiple_of(i * tile, tile), tile)
                partial[part, :, :, to] = value.reshape(n_chip, 2 * rows, tile)
                return carry

            lax.fori_loop(0, quarter // tile, down, 0)
            for rel in in_phase(part, 0):
                s_buf[part, rel - 1] = reduced(part, rel).astype(jnp.bfloat16)
                reduce_copy(part, rel).start()
        for place in range(1, bits - 1):
            for part in range(2):
                for rel in in_phase(part, place):
                    s_buf[part, rel - 1] = reduced(part, rel).astype(jnp.bfloat16)
                    reduce_copy(part, rel).start()
        for part in range(2):
            pair_sum[part] = reduced(part, 0).reshape(2, rows, quarter)
            s_core[part] = pair_sum[part, 1 - member].astype(jnp.bfloat16)
            core_copy(part).start()
        for part in range(2):
            at = pl.ds(pl.multiple_of(member * half + part * quarter, 128), quarter)
            xout[micro, :, at] = (
                xin[micro, :, at].astype(jnp.float32) + pair_sum[part, member]
            ).astype(jnp.bfloat16)
        for part in range(2):
            core_copy(part).wait()
            at = pl.ds(pl.multiple_of((1 - member) * half + part * quarter, 128), quarter)
            xout[micro, :, at] = (
                xin[micro, :, at].astype(jnp.float32) + r_core[part].astype(jnp.float32)
            ).astype(jnp.bfloat16)

        @pl.when(section < last)
        def _():
            relay_copy(micro).start()

        @pl.when(jnp.logical_and(section == last, micro < last))
        def _():
            final_copy(micro).start()

        for part in range(2):
            for rel in range(1, n_chip):
                reduce_copy(part, rel).wait_send()
        return unused

    lax.fori_loop(0, micro_count, one_micro, 0)

    @pl.when(section < last)
    def _():
        for micro in range(micro_count):
            relay_copy(micro).wait_send()
        final_copy(0).wait_recv()
        out_ref[0] = fin[...]

    @pl.when(section == last)
    def _():
        for micro in range(micro_count - 1):
            final_copy(micro).wait_send()
        out_ref[0] = xout[micro_count - 1]


def on_device(inputs, norm_gain, router_weight, gate_weight, up_weight, down_weight, routing):
    n_pp, n_ep = lax.axis_size("pp"), lax.axis_size("ep")
    micro_count, rows, width = inputs.shape
    experts = router_weight.shape[2]
    hid = gate_weight.shape[2]
    half = width // 2
    quarter = half // 2
    n_chip = n_ep // 2
    router_rows = router_weight[0].T.astype(jnp.float32)
    bf16, f32 = jnp.bfloat16, jnp.float32
    dma = pltpu.SemaphoreType.DMA
    any_spec = pl.BlockSpec(memory_space=pl.ANY)
    vmem_spec = pl.BlockSpec(memory_space=pltpu.VMEM)
    return pl.pallas_call(
        functools.partial(kernel, n_pp, n_ep, experts),
        out_shape=jax.ShapeDtypeStruct((1, rows, width), bf16),
        in_specs=[any_spec, vmem_spec, vmem_spec, any_spec, any_spec, any_spec, vmem_spec],
        out_specs=vmem_spec,
        scratch_shapes=[
            pltpu.VMEM((micro_count, rows, width), bf16),
            pltpu.VMEM((micro_count, rows, width), bf16),
            pltpu.VMEM((rows, width), bf16),
            pltpu.VMEM((2, n_ep, rows, half), bf16),
            pltpu.VMEM((n_ep, rows, 128), f32),
            pltpu.VMEM((width, hid), bf16),
            pltpu.VMEM((width, hid), bf16),
            pltpu.VMEM((2 * hid, half), bf16),
            pltpu.VMEM((n_ep * rows, hid), f32),
            pltpu.VMEM((n_ep * rows, hid), f32),
            pltpu.VMEM((n_ep * rows, hid), bf16),
            pltpu.VMEM((n_ep * rows, hid), bf16),
            pltpu.VMEM((2, n_chip, 2 * rows, quarter), f32),
            pltpu.VMEM((2, 2, rows, quarter), f32),
            pltpu.VMEM((2, n_chip - 1, 2 * rows, quarter), bf16),
            pltpu.VMEM((2, n_chip - 1, 2 * rows, quarter), bf16),
            pltpu.VMEM((2, rows, quarter), bf16),
            pltpu.VMEM((2, rows, quarter), bf16),
            dma, dma((3,)), dma((3, n_ep)), dma((3, n_ep)), dma, dma,
            dma((2, n_chip)), dma((2, n_chip)), dma((2,)), dma((2,)),
            dma((micro_count,)), dma((micro_count,)), dma((micro_count,)), dma,
        ],
        compiler_params=pltpu.CompilerParams(
            collective_id=0, has_side_effects=True, vmem_limit_bytes=60 * 1024 * 1024
        ),
    )(inputs, norm_gain, router_rows, gate_weight, up_weight, down_weight, routing[0])


def solution(mesh):
    return jax.shard_map(
        on_device,
        mesh=mesh,
        in_specs=(
            P(None, "ep", None),
            P("pp", None),
            P("pp", None, None),
            P("pp", None, "ep"),
            P("pp", None, "ep"),
            P("pp", None, "ep"),
            P("pp", None, "ep", None),
        ),
        out_specs=P("pp", "ep", None),
        check_vma=False,
    )
```

time: 476 us -> 257 us (0.54)
  Pallas kernels: 0 us -> 252 us
  waiting for transfers between devices: 226 us -> 0 us
  starting transfers between devices: 93.8 us -> 0 us
  matrix products: 81.1 us -> 0 us
  local copies, waits for them, and re-layouts: 41.9 us -> 3.03 us
  other arithmetic: 28.7 us -> 1.48 us
    pallas_call x0 -> x1, Pallas kernels: none -> 252 us  [on_device(): pl.pallas_call(functools.partial(kernel, n_pp, n_ep, experts), out_shape=...]
    all_to_all x14 -> x0, waiting for transfers between devices: 172 us -> none  [the longest x7 86.9 us: moe_layer(): lax.all_to_all(outgoing, 'ep', split_axis=0, concat_axis=0, tiled=True)]
    dot_general x49 -> x0, matrix products: 81.1 us -> none  [the longest x7 30.5 us: expert_rows(): jnp.einsum('smd,dh->smh', received, gate_block, preferred_element_type=jn...]
    all_to_all x14 -> x0, starting transfers between devices: 65 us -> none  [the longest x7 34.3 us: expert_rows(): lax.all_to_all(outcome, 'ep', split_axis=0, concat_axis=0, tiled=True)]
    ppermute x28 -> x0, waiting for transfers between devices: 53.4 us -> none  [the longest x14 51.1 us: from_behind(): lax.ppermute(value, axis, [(source, source + steps) for source in range(f...]
    ppermute x28 -> x0, starting transfers between devices: 28.9 us -> none  [the longest x14 22.4 us: from_behind(): lax.ppermute(value, axis, [(source, source + steps) for source in range(f...]
    reduce_sum x28 -> x0, other arithmetic: 18 us -> none  [the longest x7 8.67 us: moe_layer(): combined = jnp.sum(mixing[:, :, None] * picks.astype(jnp.float32), axis=1)]
    gather x7 -> x0, local copies, waits for them, and re-layouts: 10.5 us -> none  [moe_layer(): halves[expert_of, :, slot_index, :].reshape(tok_rows, top_count, width)]
  transfers between devices with their start and end apart: 42 -> 0, of which waited for: 28 -> 0; matrix products, arithmetic and copies ran while one was open for 23% -> 0% of each run, Pallas kernels for 0% -> 0%
where the time goes in v1:
time: 257 us
  Pallas kernels  252 us (98%)
  local copies, waits for them, and re-layouts  3.03 us (1%)
    pallas_call x1, Pallas kernels, on_device(): pl.pallas_call(functools.partial(kernel, n_pp, n_ep, experts), out_shape=...  252 us

profile of v1, /device:TPU:27, one launch (start us, length us, event | category | flops | bytes accessed | tf_op | source)
XLA Modules:
  0.0 256.6 jit_solution(11326268875733525673)
XLA Ops:
  0.0 1.4 copy.9.routing_ref
  1.4 1.5 convert_bitcast_fusion.router_ref
  2.9 252.1 %shard_map.73 = bf16[1,16,7168]{2,1,0:T(8,128)(2,1)} custom-call(bf16[4,16,7168]{2,1,0:T(8,128)(2,1)} %inputs_ref.1, f32[1,7168]{1,0:T(1,128)} %gain_ref.1, f32[4,7168]{1,0:T(4,128)} %convert_bitcast_fusion.router_ref, bf16[1,7168,512]{2,1,0:T(8,128)(2,1)} %gate_hbm.1, bf16[1,7168,512]{2,1,0:T(8,128)(2,1)} %up_hbm.1, bf16[1,1024,3584]{2,1,0:T(8,128)(2,1)} %down_hbm.1, ...), custom_call_target="tpu_custom_call" | custom-call | tf_op jit(solution)/shard_map/pallas_call | solution.py:312
  255.0 1.6 copy.13

commit v2 on v1

v2 whole, which is shorter than its diff:
```python
import functools

import jax
import jax.numpy as jnp
from jax import lax
from jax.experimental import pallas as pl
from jax.experimental.pallas import tpu as pltpu
from jax.sharding import PartitionSpec as P

routed_scale = 2.5
norm_epsilon = 1e-06


def cut(size, wanted=4, unit=256):
    units = size // unit
    shares = [units // wanted + (k < units % wanted) for k in range(wanted)]
    starts = [sum(shares[:k]) for k in range(wanted)]
    return [(start * unit, share * unit) for start, share in zip(starts, shares)]


def kernel(
    n_pp, n_ep, experts,
    inputs_ref, gain_ref, router_ref, gate_hbm, up_hbm, down_hbm, routing_ref,
    out_ref,
    xin, xout, fin, tokens, mixes, wg, wu, wd, acc_g, acc_u, squares, hid_own, hid_par, partial, pair_sum,
    s_buf, r_buf, s_core, r_core,
    load_sem, weight_sem, tok_send, tok_recv, hid_send, hid_recv, red_send, red_recv,
    core_send, core_recv, x_send, x_recv, fin_send, fin_recv,
):
    section = lax.axis_index("pp")
    me = lax.axis_index("ep")
    member, chip = me % 2, me // 2
    last = n_pp - 1
    bits = n_ep.bit_length() - 1
    micro_count, unused, rows, half = xin.shape
    width = 2 * half
    parts = cut(half)
    n_part = len(parts)
    n_chip = n_ep // 2
    all_rows = n_ep * rows
    hid = wg.shape[1]

    def at_bit(b):
        return me + (1 << b) - 2 * (1 << b) * ((me // (1 << b)) % 2)

    def flip(value, mask):
        for b in range(bits):
            if mask >> b & 1:
                value = value + (1 << b) - 2 * (1 << b) * ((value // (1 << b)) % 2)
        return value

    copies = [
        pltpu.make_async_copy(gate_hbm.at[0], wg, weight_sem.at[0]),
        pltpu.make_async_copy(up_hbm.at[0], wu, weight_sem.at[1]),
        pltpu.make_async_copy(down_hbm.at[0], wd, weight_sem.at[2]),
    ]
    loads = [
        pltpu.make_async_copy(
            inputs_ref.at[:, :, pl.ds(side * half, half)], xin.at[:, side], load_sem.at[side]
        )
        for side in range(2)
    ]

    @pl.when(section == 0)
    def _():
        for load in loads:
            load.start()

    for copy in copies:
        copy.start()

    barrier = pltpu.get_barrier_semaphore()
    for b in range(bits):
        pl.semaphore_signal(
            barrier, inc=1, device_id={"ep": at_bit(b)}, device_id_type=pl.DeviceIdType.MESH
        )
    for step in range(1, n_pp):
        pl.semaphore_signal(
            barrier, inc=1, device_id={"pp": (section + step) % n_pp},
            device_id_type=pl.DeviceIdType.MESH,
        )
    pl.semaphore_wait(barrier, bits + n_pp - 1)

    @pl.when(section == 0)
    def _():
        for load in loads:
            load.wait()

    chip_bits = list(range(1, bits))
    gather_orders = [chip_bits[:: 1 - 2 * (p % 2)] + [0] for p in range(n_part)] + [chip_bits + [0]]

    def columns(part):
        return pl.ds(parts[part][0], parts[part][1])

    def token_ref(stream, source):
        if stream == n_part:
            return mixes.at[source]
        return tokens.at[:, source, :, columns(stream)]

    def token_copy(stream, rel, micro):
        order = gather_orders[stream]
        hop = [b for b in order if rel >> b & 1][-1]
        before = rel ^ (1 << hop)
        source = flip(me, before)
        src_ref = token_ref(stream, source)
        if before == 0 and stream < n_part:
            src_ref = xin.at[micro, :, :, columns(stream)]
        return pltpu.make_async_remote_copy(
            src_ref=src_ref, dst_ref=token_ref(stream, source),
            send_sem=tok_send.at[stream, rel], recv_sem=tok_recv.at[stream, rel],
            device_id={"ep": at_bit(hop)}, device_id_type=pl.DeviceIdType.MESH,
        )

    def token_arrival(stream, rel):
        ref = token_ref(stream, flip(me, rel))
        pltpu.make_async_remote_copy(
            src_ref=ref, dst_ref=ref,
            send_sem=tok_send.at[stream, rel], recv_sem=tok_recv.at[stream, rel],
            device_id={"ep": at_bit(0)}, device_id_type=pl.DeviceIdType.MESH,
        ).wait_recv()

    def onward(stream, rel):
        order = gather_orders[stream]
        start = max([order.index(b) for b in range(bits) if rel >> b & 1], default=-1) + 1
        return [rel | 1 << b for b in order[start:]]

    reduce_orders = [list(range(bits - 1))[:: 1 - 2 * (p % 2)] for p in range(n_part)]

    def first_place(part, rel):
        return min(i for i, b in enumerate(reduce_orders[part]) if rel >> b & 1)

    def reduce_copy(part, rel):
        hop = reduce_orders[part][first_place(part, rel)]
        return pltpu.make_async_remote_copy(
            src_ref=s_buf.at[rel - 1, :, columns(part)], dst_ref=r_buf.at[rel - 1, :, columns(part)],
            send_sem=red_send.at[part, rel], recv_sem=red_recv.at[part, rel],
            device_id={"ep": at_bit(hop + 1)}, device_id_type=pl.DeviceIdType.MESH,
        )

    def reduced(part, rel):
        place = len(reduce_orders[part]) if rel == 0 else first_place(part, rel)
        value = partial[flip(me, rel << 1) // 2, :, columns(part)]
        for b in reduce_orders[part][:place]:
            reduce_copy(part, rel | 1 << b).wait_recv()
            value = value + r_buf[(rel | 1 << b) - 1, :, columns(part)].astype(jnp.float32)
        return value

    def in_phase(part, place):
        found = [q for q in range(1, n_chip) if first_place(part, q) == place]
        return sorted(found, key=lambda q: -bin(q).count("1"))

    hid_copy = pltpu.make_async_remote_copy(
        src_ref=hid_own, dst_ref=hid_par, send_sem=hid_send, recv_sem=hid_recv,
        device_id={"ep": at_bit(0)}, device_id_type=pl.DeviceIdType.MESH,
    )

    def core_copy(part):
        return pltpu.make_async_remote_copy(
            src_ref=s_core.at[:, columns(part)], dst_ref=r_core.at[:, columns(part)],
            send_sem=core_send.at[part], recv_sem=core_recv.at[part],
            device_id={"ep": at_bit(0)}, device_id_type=pl.DeviceIdType.MESH,
        )

    def relay_copy(micro, part):
        return pltpu.make_async_remote_copy(
            src_ref=xout.at[micro, :, :, columns(part)], dst_ref=xin.at[micro, :, :, columns(part)],
            send_sem=x_send.at[micro, part], recv_sem=x_recv.at[micro, part],
            device_id={"pp": (section + 1) % n_pp}, device_id_type=pl.DeviceIdType.MESH,
        )

    def final_copy(micro):
        return pltpu.make_async_remote_copy(
            src_ref=xout.at[micro], dst_ref=fin,
            send_sem=fin_send.at[micro], recv_sem=fin_recv,
            device_id={"pp": micro}, device_id_type=pl.DeviceIdType.MESH,
        )

    def one_micro(micro, unused):
        acc_g[...] = jnp.zeros_like(acc_g)
        acc_u[...] = jnp.zeros_like(acc_u)
        squares[...] = jnp.zeros_like(squares)
        tile = 256
        single = [r for r in range(1, n_ep) if r & 1 == 0 and bin(r).count("1") == 1]
        others = sorted(
            [r for r in range(1, n_ep) if r not in single],
            key=lambda r: (bin(r >> 1).count("1"), r & 1),
        )

        def arrive(stream, rels):
            for rel in rels:
                token_arrival(stream, rel)
                for later in onward(stream, rel):
                    token_copy(stream, later, micro).start()

        def project_part(part):
            start, size = parts[part]

            def project(i, carry):
                side = i // (size // tile)
                at = pl.multiple_of(start + (i - side * (size // tile)) * tile, tile)
                where = pl.ds(pl.multiple_of(side * half + at, tile), tile)
                block = tokens[side, :, :, pl.ds(at, tile)].reshape(all_rows, tile)
                block = block.astype(jnp.float32)
                square = block * block
                squares[...] += functools.reduce(
                    lambda a, b: a + b, [square[:, k : k + 128] for k in range(0, tile, 128)]
                )
                block = (block * gain_ref[:, where]).astype(jnp.bfloat16)
                acc_g[...] += jnp.dot(block, wg[where, :], preferred_element_type=jnp.float32)
                acc_u[...] += jnp.dot(block, wu[where, :], preferred_element_type=jnp.float32)
                return carry

            lax.fori_loop(0, 2 * size // tile, project, 0)

        for step in range(n_part + 2):
            if step < n_part:

                @pl.when(section > 0)
                def _():
                    relay_copy(micro, step).wait_recv()

                for rel in onward(step, 0):
                    token_copy(step, rel, micro).start()
                tokens[:, me, :, columns(step)] = xin[micro, :, :, columns(step)]
            if step == n_part - 1:
                sides = [xin[micro, side].astype(jnp.float32) for side in range(2)]
                total = sum(jnp.sum(v * v, axis=1, keepdims=True) for v in sides)
                scale = lax.rsqrt(total / width + norm_epsilon)
                normed = [
                    (sides[k] * scale * gain_ref[:, k * half : (k + 1) * half])
                    .astype(jnp.bfloat16)
                    .astype(jnp.float32)
                    for k in range(2)
                ]
                routes = routing_ref[micro]
                top = routes.shape[1]
                picked = [jnp.zeros((rows, 1), jnp.float32) for k in range(top)]
                for e in range(experts):
                    logit = sum(
                        jnp.sum(
                            normed[k] * router_ref[e : e + 1, k * half : (k + 1) * half],
                            axis=1, keepdims=True,
                        )
                        for k in range(2)
                    )
                    score = jax.nn.sigmoid(logit)
                    for k in range(top):
                        picked[k] = picked[k] + jnp.where(routes[:, k : k + 1] == e, score, 0.0)
                total = functools.reduce(lambda a, b: a + b, picked)
                lanes = lax.broadcasted_iota(jnp.int32, (rows, 128), 1)
                mix = jnp.zeros((rows, 128), jnp.float32)
                for k in range(top):
                    share = routed_scale * picked[k] / total
                    mix = mix + jnp.where(lanes == routes[:, k : k + 1], share, 0.0)
                mixes[me] = mix
                for rel in onward(n_part, 0):
                    token_copy(n_part, rel, micro).start()
            if 1 <= step <= n_part:
                arrive(step - 1, single)
            if step >= 2:
                arrive(step - 2, others)
                if step == 2:

                    @pl.when(micro == 0)
                    def _():
                        copies[0].wait()
                        copies[1].wait()

                if step == n_part + 1:
                    arrive(n_part, single + others)
                project_part(step - 2)

        scale = lax.rsqrt(
            jnp.sum(squares[...], axis=1, keepdims=True) / width + norm_epsilon
        )
        gate_proj = acc_g[...] * scale
        hid_own[...] = (
            gate_proj / (1.0 + jnp.exp(-gate_proj)) * (acc_u[...] * scale)
        ).astype(jnp.bfloat16)
        hid_copy.start()
        for rel in range(1, n_ep):
            for stream in range(n_part + 1):
                token_copy(stream, rel, micro).wait_send()

        @pl.when(micro == 0)
        def _():
            copies[2].wait()

        lane3 = lax.broadcasted_iota(jnp.int32, (n_ep, rows, 128), 2)
        mix_all = jnp.sum(
            jnp.where(lane3 == chip, mixes[...], 0.0), axis=2, keepdims=True
        ).reshape(all_rows, 1)
        hid_copy.wait()

        own_rows = pl.ds(pl.multiple_of(member * hid, hid), hid)
        par_rows = pl.ds(pl.multiple_of((1 - member) * hid, hid), hid)

        def send_reduced(part, rel):
            s_buf[rel - 1, :, columns(part)] = reduced(part, rel).astype(jnp.bfloat16)
            reduce_copy(part, rel).start()

        for part in range(n_part):

            def down(i, carry, part=part):
                at = pl.ds(pl.multiple_of(parts[part][0] + i * tile, tile), tile)
                value = jnp.dot(hid_own[...], wd[own_rows, at], preferred_element_type=jnp.float32)
                value += jnp.dot(hid_par[...], wd[par_rows, at], preferred_element_type=jnp.float32)
                value = value * mix_all
                partial[:, :, at] = value.reshape(n_chip, 2 * rows, tile)
                return carry

            lax.fori_loop(0, parts[part][1] // tile, down, 0)
            for rel in in_phase(part, 0):
                send_reduced(part, rel)
        for step in range(n_part + 2):
            if step < n_part:
                for place in range(1, bits - 1):
                    for rel in in_phase(step, place):
                        send_reduced(step, rel)
            if 1 <= step <= n_part:
                part = step - 1
                at = columns(part)
                pair_sum[:, :, at] = reduced(part, 0).reshape(2, rows, parts[part][1])
                s_core[:, at] = pair_sum[1 - member, :, at].astype(jnp.bfloat16)
                core_copy(part).start()
                xout[micro, member, :, at] = (
                    xin[micro, member, :, at].astype(jnp.float32) + pair_sum[member, :, at]
                ).astype(jnp.bfloat16)
            if step >= 2:
                part = step - 2
                at = columns(part)
                core_copy(part).wait()
                xout[micro, 1 - member, :, at] = (
                    xin[micro, 1 - member, :, at].astype(jnp.float32)
                    + r_core[:, at].astype(jnp.float32)
                ).astype(jnp.bfloat16)

                @pl.when(section < last)
                def _():
                    relay_copy(micro, part).start()

        @pl.when(jnp.logical_and(section == last, micro < last))
        def _():
            final_copy(micro).start()

        for part in range(n_part):
            for rel in range(1, n_chip):
                reduce_copy(part, rel).wait_send()
        return unused

    lax.fori_loop(0, micro_count, one_micro, 0)

    @pl.when(section < last)
    def _():
        for micro in range(micro_count):
            for part in range(n_part):
                relay_copy(micro, part).wait_send()
        final_copy(0).wait_recv()
        for side in range(2):
            out_ref[0, :, pl.ds(side * half, half)] = fin[side]

    @pl.when(section == last)
    def _():
        for micro in range(micro_count - 1):
            final_copy(micro).wait_send()
        for side in range(2):
            out_ref[0, :, pl.ds(side * half, half)] = xout[micro_count - 1, side]


def on_device(inputs, norm_gain, router_weight, gate_weight, up_weight, down_weight, routing):
    n_pp, n_ep = lax.axis_size("pp"), lax.axis_size("ep")
    micro_count, rows, width = inputs.shape
    experts = router_weight.shape[2]
    hid = gate_weight.shape[2]
    half = width // 2
    n_part = len(cut(half))
    n_chip = n_ep // 2
    router_rows = router_weight[0].T.astype(jnp.float32)
    bf16, f32 = jnp.bfloat16, jnp.float32
    dma = pltpu.SemaphoreType.DMA
    any_spec = pl.BlockSpec(memory_space=pl.ANY)
    vmem_spec = pl.BlockSpec(memory_space=pltpu.VMEM)
    return pl.pallas_call(
        functools.partial(kernel, n_pp, n_ep, experts),
        out_shape=jax.ShapeDtypeStruct((1, rows, width), bf16),
        in_specs=[any_spec, vmem_spec, vmem_spec, any_spec, any_spec, any_spec, vmem_spec],
        out_specs=vmem_spec,
        scratch_shapes=[
            pltpu.VMEM((micro_count, 2, rows, half), bf16),
            pltpu.VMEM((micro_count, 2, rows, half), bf16),
            pltpu.VMEM((2, rows, half), bf16),
            pltpu.VMEM((2, n_ep, rows, half), bf16),
            pltpu.VMEM((n_ep, rows, 128), f32),
            pltpu.VMEM((width, hid), bf16),
            pltpu.VMEM((width, hid), bf16),
            pltpu.VMEM((2 * hid, half), bf16),
            pltpu.VMEM((n_ep * rows, hid), f32),
            pltpu.VMEM((n_ep * rows, hid), f32),
            pltpu.VMEM((n_ep * rows, 128), f32),
            pltpu.VMEM((n_ep * rows, hid), bf16),
            pltpu.VMEM((n_ep * rows, hid), bf16),
            pltpu.VMEM((n_chip, 2 * rows, half), f32),
            pltpu.VMEM((2, rows, half), f32),
            pltpu.VMEM((n_chip - 1, 2 * rows, half), bf16),
            pltpu.VMEM((n_chip - 1, 2 * rows, half), bf16),
            pltpu.VMEM((rows, half), bf16),
            pltpu.VMEM((rows, half), bf16),
            dma((2,)), dma((3,)), dma((n_part + 1, n_ep)), dma((n_part + 1, n_ep)), dma, dma,
            dma((n_part, n_chip)), dma((n_part, n_chip)), dma((n_part,)), dma((n_part,)),
            dma((micro_count, n_part)), dma((micro_count, n_part)), dma((micro_count,)), dma,
        ],
        compiler_params=pltpu.CompilerParams(
            collective_id=0, has_side_effects=True, vmem_limit_bytes=60 * 1024 * 1024
        ),
    )(inputs, norm_gain, router_rows, gate_weight, up_weight, down_weight, routing[0])


def solution(mesh):
    return jax.shard_map(
        on_device,
        mesh=mesh,
        in_specs=(
            P(None, "ep", None),
            P("pp", None),
            P("pp", None, None),
            P("pp", None, "ep"),
            P("pp", None, "ep"),
            P("pp", None, "ep"),
            P("pp", None, "ep", None),
        ),
        out_specs=P("pp", "ep", None),
        check_vma=False,
    )
```

time: 257 us -> 283 us (1.10)
  Pallas kernels: 252 us -> 278 us
    pallas_call x1, Pallas kernels: 252 us -> 278 us  [on_device(): pl.pallas_call(functools.partial(kernel, n_pp, n_ep, experts), out_shape=...]
where the time goes in v2:
time: 283 us
  Pallas kernels  278 us (98%)
  local copies, waits for them, and re-layouts  3.03 us (1%)
    pallas_call x1, Pallas kernels, on_device(): pl.pallas_call(functools.partial(kernel, n_pp, n_ep, experts), out_shape=...  278 us

profile of v2, /device:TPU:27, one launch (start us, length us, event | category | flops | bytes accessed | tf_op | source)
XLA Modules:
  0.0 282.8 jit_solution(18050170385786141875)
XLA Ops:
  0.0 1.4 copy.9.routing_ref
  1.4 1.5 convert_bitcast_fusion.router_ref
  2.9 278.3 %shard_map.73 = bf16[1,16,7168]{2,1,0:T(8,128)(2,1)} custom-call(bf16[4,16,7168]{2,1,0:T(8,128)(2,1)} %inputs_ref.1, f32[1,7168]{1,0:T(1,128)} %gain_ref.1, f32[4,7168]{1,0:T(4,128)} %convert_bitcast_fusion.router_ref, bf16[1,7168,512]{2,1,0:T(8,128)(2,1)} %gate_hbm.1, bf16[1,7168,512]{2,1,0:T(8,128)(2,1)} %up_hbm.1, bf16[1,1024,3584]{2,1,0:T(8,128)(2,1)} %down_hbm.1, ...), custom_call_target="tpu_custom_call" | custom-call | tf_op jit(solution)/shard_map/pallas_call | solution.py:383
  281.1 1.6 copy.13

commit v3 on v1

--- a/solution.py
+++ b/solution.py
@@ -199,7 +199,7 @@
 
         acc_g[...] = jnp.zeros_like(acc_g)
         acc_u[...] = jnp.zeros_like(acc_u)
-        depth = 512
+        depth = half // 2
         for stream in range(2):
 
             def project(i, carry, stream=stream):
@@ -228,7 +228,7 @@
         ).reshape(all_rows, 1)
         hid_copy.wait()
 
-        tile = 256
+        tile = quarter
         own_rows = pl.ds(pl.multiple_of(member * hid, hid), hid)
         par_rows = pl.ds(pl.multiple_of((1 - member) * hid, hid), hid)
         for part in range(2):

time: 257 us -> 231 us (0.90)
  Pallas kernels: 252 us -> 227 us
    pallas_call x1, Pallas kernels: 252 us -> 227 us  [on_device(): pl.pallas_call(functools.partial(kernel, n_pp, n_ep, experts), out_shape=...]
where the time goes in v3:
time: 231 us
  Pallas kernels  227 us (98%)
  local copies, waits for them, and re-layouts  3.03 us (1%)
    pallas_call x1, Pallas kernels, on_device(): pl.pallas_call(functools.partial(kernel, n_pp, n_ep, experts), out_shape=...  227 us

profile of v3, /device:TPU:27, one launch (start us, length us, event | category | flops | bytes accessed | tf_op | source)
XLA Modules:
  0.0 231.1 jit_solution(4190555105942440539)
XLA Ops:
  0.0 1.4 copy.9.routing_ref
  1.4 1.5 convert_bitcast_fusion.router_ref
  2.9 226.6 %shard_map.73 = bf16[1,16,7168]{2,1,0:T(8,128)(2,1)} custom-call(bf16[4,16,7168]{2,1,0:T(8,128)(2,1)} %inputs_ref.1, f32[1,7168]{1,0:T(1,128)} %gain_ref.1, f32[4,7168]{1,0:T(4,128)} %convert_bitcast_fusion.router_ref, bf16[1,7168,512]{2,1,0:T(8,128)(2,1)} %gate_hbm.1, bf16[1,7168,512]{2,1,0:T(8,128)(2,1)} %up_hbm.1, bf16[1,1024,3584]{2,1,0:T(8,128)(2,1)} %down_hbm.1, ...), custom_call_target="tpu_custom_call" | custom-call | tf_op jit(solution)/shard_map/pallas_call | solution.py:312
  229.5 1.6 copy.13
